TPU v7x, 256 devices: a whole 4x4x8 slice. The times are simulated.
256 devices in a mesh: mem: 32 (over y, z_lo, core), tile: 8 (over x, z_hi).
Axes of the slice: x: 4, y: 4, z: 8 (z_hi: 2, z_lo: 4; z = z_hi * 4 + z_lo), core: 2. Of those that a mesh axis runs over, the one named last changes fastest.
Arguments:
- weights: float32 [32, 8, 128, 512], P('mem', None, 'tile'), may hold values from -3 to 3
- perturb: bfloat16 [32, 8, 128, 512], P('mem', None, 'tile'), may hold values from -6 to 6
- coef_lon: float32 [8, 128, 512], P(None, 'tile'), may hold values from 0.01 to 0.09
- coef_lat: float32 [8, 128, 512], P(None, 'tile'), may hold values from 0.2 to 0.4
- obs_value: float32 [16384, 128], P(('mem', 'tile')), may hold values from -6 to 6
- obs_weight: float32 [16384, 128], P(('mem', 'tile')), may hold values from 0.25 to 4
- obs_segment: int32 [16384], P(('mem', 'tile')), may hold values from 0 to 511
- obs_kind: int32 [16384], P(('mem', 'tile')), may hold values from 0 to 3
- obs_target: int32 [16384, 1], P(('mem', 'tile')), may hold values from 0 to 7; in each aligned block of 64 rows (0 to 63, 64 to 127, ...) at most 16 rows name the same one
- obs_count: int32 [256], P(('mem', 'tile')), may hold values from 1 to 64, 8192 in all
- operators: float32 [4, 128, 128], replicated, may hold values from -0.5 to 0.5
Outputs:
- increment: float32 [8, 128, 512], P(None, 'tile')
- gradient: float32 [32, 8, 128, 512], P('mem', None, 'tile')
Inputs may be any that keep to these rules, and one draw needn't show every extreme that they name: `obs_target`: in the 64 rows of one owner no tile is named by more than 16 rows. The first obs_count slots of an owner hold observations, the others are empty and ignored.
All inputs are finite; a program needn't handle non-finite values. No bound on the sum of `obs_count` on one device may be relied on, other than what follows from the above.
Results may differ from a plain program's by a relative error of at most 0.0003.
Values sent between devices are 32-bit elements; how exact they have to be, the bound alone decides.
A program may use at most 64 MiB of HBM per device.

v0:
```python
import math
import jax
import jax.numpy as jnp
from jax import lax
from jax.sharding import PartitionSpec as P

SEG = 128
SWEEPS = 16


def extended_2(shard, sides, width):
    for axis, dim in sides:
        peers, length = (lax.axis_size(axis), shard.shape[dim])
        up = [(i, (i + 1) % peers) for i in range(peers - 1)]
        down = [(j, i) for i, j in up]
        last = lax.slice_in_dim(shard, length - width, length, axis=dim)
        first = lax.slice_in_dim(shard, 0, width, axis=dim)
        before = lax.ppermute(last, axis, up)
        after = lax.ppermute(first, axis, down)
        shard = jnp.concatenate([before, shard, after], axis=dim)
    return shard


def advance(current, padded, coef_lon, coef_lat):
    zonal_term = jnp.roll(current, 1, 2) + jnp.roll(current, -1, 2) - 2.0 * current
    across = padded[:, 2:] + padded[:, :-2] - 2.0 * current
    return current + coef_lon * zonal_term + coef_lat * across


def retreat(current, padded_lat, coef_lon, coef_lat):
    flux_lon = coef_lon * current
    retain = 1.0 - 2.0 * coef_lon - 2.0 * coef_lat
    return (
        retain * current
        + jnp.roll(flux_lon, 1, 2)
        + jnp.roll(flux_lon, -1, 2)
        + padded_lat[:, 2:]
        + padded_lat[:, :-2]
    )


def smooth_forward(current, coef_lon, coef_lat):
    for sweep_index in range(SWEEPS):
        padded = extended_2(current, (("tile", 1),), 1)
        current = advance(current, padded, coef_lon, coef_lat)
    return current


def smooth_adjoint(current, coef_lon, coef_lat):
    for sweep_index in range(SWEEPS):
        padded = extended_2(coef_lat * current, (("tile", 1),), 1)
        current = retreat(current, padded, coef_lon, coef_lat)
    return current


def observe(blocks, operators, kinds, values, precisions):
    images = jnp.einsum("bj,kij->kbi", blocks, operators, precision=lax.Precision.HIGHEST)
    choose = (kinds[None, :] == jnp.arange(operators.shape[0])[:, None]).astype(jnp.float32)[
        :, :, None
    ]
    modelled = jnp.sum(choose * images, 0)
    misfit = precisions * (modelled - values)
    return jnp.einsum(
        "kbi,kij->bj", choose * misfit[None], operators, precision=lax.Precision.HIGHEST
    )


def shards(
    weights,
    perturb,
    coef_lon,
    coef_lat,
    obs_value,
    obs_weight,
    obs_segment,
    obs_kind,
    obs_target,
    obs_count,
    operators,
):
    tiles = lax.axis_size("tile")
    scale = 1.0 / math.sqrt(lax.axis_size("mem"))
    member_weights = weights[0]
    member_perturb = perturb[0].astype(jnp.float32)
    product = member_perturb * smooth_forward(member_weights, coef_lon, coef_lat)
    summed = lax.psum(product, "mem")
    increment = summed * scale
    table = increment.reshape(-1, SEG)
    slots = obs_value.shape[0]
    capacity = 2 * slots // tiles
    live = jnp.arange(slots) < obs_count[0]
    target = obs_target[:, 0]
    onehot = (target[:, None] == jnp.arange(tiles)[None, :]).astype(jnp.int32)
    earlier = jnp.cumsum(onehot, 0) - onehot
    position = target * capacity + jnp.sum(earlier * onehot, 1)
    live_weight = obs_weight * live.astype(jnp.float32)[:, None]
    request = (
        jnp.full((tiles * capacity,), -1, jnp.int32)
        .at[position]
        .set(jnp.where(live, obs_segment, -1))
    )
    asked = lax.all_to_all(
        request.reshape(tiles, capacity), "tile", split_axis=0, concat_axis=0, tiled=True
    ).reshape(-1)
    valid = (asked >= 0).astype(jnp.float32)[:, None]
    index = jnp.maximum(asked, 0)
    found = table[index] * valid
    answered = lax.all_to_all(
        found.reshape(tiles, capacity, SEG), "tile", split_axis=0, concat_axis=0, tiled=True
    ).reshape(-1, SEG)
    adjoint = observe(answered[position], operators, obs_kind, obs_value, live_weight)
    outgoing = jnp.zeros((tiles * capacity, SEG), jnp.float32).at[position].set(adjoint)
    returned = lax.all_to_all(
        outgoing.reshape(tiles, capacity, SEG), "tile", split_axis=0, concat_axis=0, tiled=True
    ).reshape(-1, SEG)
    local_table = jnp.zeros_like(table).at[index].add(returned)
    adjoint_table = lax.psum(local_table, "mem")
    adjoint_field = adjoint_table.reshape(increment.shape)
    backward = smooth_adjoint(member_perturb * adjoint_field, coef_lon, coef_lat)
    member_gradient = member_weights + backward * scale
    return (increment, member_gradient[None])


def solution(mesh):
    placed = (
        P("mem", None, "tile", None),
        P("mem", None, "tile", None),
        P(None, "tile", None),
        P(None, "tile", None),
        P(("mem", "tile"), None),
        P(("mem", "tile"), None),
        P(("mem", "tile")),
        P(("mem", "tile")),
        P(("mem", "tile"), None),
        P(("mem", "tile")),
        P(),
    )
    return jax.shard_map(
        shards,
        mesh=mesh,
        in_specs=placed,
        out_specs=(P(None, "tile", None), P("mem", None, "tile", None)),
        check_vma=False,
    )
```

profile of v0, /device:TPU:6, one launch (start us, length us, event | category | flops | bytes accessed | tf_op | source)
XLA Modules:
  0.0 1062.2 jit_solution(6415799808595329105)
XLA Ops:
  12.3 11.4 %all-to-all-start = ((s32[8,1,16]{2,1,0:T(1,128)}), s32[8,1,16]{2,1,0:T(1,128)S(1)}, u32[]{:S(2)}, u32[]{:S(2)}) async-start(s32[8,1,16]{2,1,0:T(1,128)} %bitcast.7), calls=%async_computation | async-start | bytes 8192 | tf_op jit(solution)/shard_map/all_to_all | solution.py:102
  119.2 7.8 collective-permute-start.13
  132.0 7.8 collective-permute-start.15
  144.9 7.8 collective-permute-start.17
  170.6 7.8 collective-permute-start.21
  183.3 7.8 collective-permute-start.23
  196.1 7.8 collective-permute-start.25
  208.9 7.8 collective-permute-start.27
  221.6 7.8 collective-permute-start.29
  234.4 8.0 collective-permute-start.31
  246.0 278.6 %all-reduce.3.cloned.1.call-done = f32[8,16,512]{2,1,0:T(8,128)} async-done(((f32[8,16,512]{2,1,0:T(8,128)}), f32[8,16,512]{2,1,0:T(8,128)}) %all-reduce.3.cloned.1.call-update) | async-done | bytes 262160 | tf_op jit(solution)/shard_map/psum | solution.py:86
  527.6 9.8 all-to-all-start.1
  537.4 8.3 all-to-all-done.1
  548.2 12.6 %all_to_all.19 = f32[8,16,128]{2,1,0:T(8,128)S(1)} all-to-all(f32[8,16,128]{2,1,0:T(8,128)S(1)} %bitcast.56), channel_id=1, replica_groups=mesh['mem'=32,'tile'=8] {'tile'}, dimensions={0} | all-to-all | bytes 131072 | tf_op jit(solution)/shard_map/all_to_all | solution.py:113
  563.0 271.7 %all-reduce.5.cloned.1.call-done = f32[8,16,512]{2,1,0:T(8,128)} async-done(((f32[8,16,512]{2,1,0:T(8,128)}), f32[8,16,512]{2,1,0:T(8,128)}) %all-reduce.5.cloned.1.call-update) | async-done | bytes 262160 | tf_op jit(solution)/shard_map/psum | solution.py:117
  845.8 8.3 collective-permute-done.33
  856.3 8.0 collective-permute-start.35
  886.7 7.8 collective-permute-start.39
  942.4 7.8 collective-permute-start.47
  968.0 7.8 collective-permute-start.51
  980.7 7.8 collective-permute-start.53
  1006.0 7.8 collective-permute-start.57
  1018.7 7.8 collective-permute-start.59
  1031.3 7.8 collective-permute-start.61
  (304 shorter events, 311.9 us)
Async XLA Ops:
  12.3 23.8 %all-to-all-start = ((s32[8,1,16]{2,1,0:T(1,128)}), s32[8,1,16]{2,1,0:T(1,128)S(1)}, u32[]{:S(2)}, u32[]{:S(2)}) async-start(s32[8,1,16]{2,1,0:T(1,128)} %bitcast.7), calls=%async_computation | async-start | bytes 8192 | tf_op jit(solution)/shard_map/all_to_all | solution.py:102
  23.7 500.8 %all-reduce.3.cloned.1.call-start = ((), (), s32[]{:S(2)}) async-start(), calls=%async_computation.3 | async-start | bytes 524288 | tf_op jit(solution)/shard_map/psum | solution.py:86
  24.7 11.5 %collective-permute-start = (f32[8,1,512]{2,1,0:T(1,128)S(1)}, f32[8,1,512]{2,1,0:T(1,128)S(1)}, u32[]{:S(2)}, u32[]{:S(2)}) collective-permute-start(f32[8,1,512]{2,1,0:T(1,128)S(1)} %get-tuple-element.225), channel_id=1, source_target_pairs={{1,0},{2,1},{3,2},{4,3},{5,4},{6,5},{7,6},{9,8},{10,9},{11,10},{12... | collective-permute-start | bytes 49160 | tf_op jit(solution)/shard_map/ppermute | solution.py:19
  32.3 10.4 collective-permute-start.1
  45.4 10.5 collective-permute-start.3
  62.9 10.4 collective-permute-start.5
  76.0 10.4 collective-permute-start.7
  93.4 10.4 collective-permute-start.9
  106.5 10.4 collective-permute-start.11
  119.2 10.4 collective-permute-start.13
  132.0 10.6 collective-permute-start.15
  157.8 10.4 collective-permute-start.19
  170.6 10.4 collective-permute-start.21
  183.3 10.4 collective-permute-start.23
  234.4 10.6 collective-permute-start.31
  527.6 18.1 %all-to-all-start.1 = ((f32[8,16,128]{2,1,0:T(8,128)}), f32[8,16,128]{2,1,0:T(8,128)S(1)}, u32[]{:S(2)}, u32[]{:S(2)}) async-start(f32[8,16,128]{2,1,0:T(8,128)} %broadcast_multiply_fusion.1), calls=%async_computation.1 | async-start | bytes 131072 | tf_op jit(solution)/shard_map/all_to_all | solution.py:108
  537.4 297.4 %all-reduce.5.cloned.1.call-start = ((), (), s32[]{:S(2)}) async-start(), calls=%async_computation.4 | async-start | bytes 524288 | tf_op jit(solution)/shard_map/psum | solution.py:117
  843.6 10.5 collective-permute-start.33
  856.3 10.5 collective-permute-start.35
  874.1 10.4 collective-permute-start.37
  955.3 10.4 collective-permute-start.49
  968.0 10.4 collective-permute-start.51
  1006.0 10.4 collective-permute-start.57
  1018.7 10.4 collective-permute-start.59
  (54 other events, 1047.4 us)
Sparse Core Ops, SparseCore 0:
  246.1 278.4 all-reduce.2
  563.1 271.5 all-reduce.4
where the time goes:
time: 1070 us; the launch traced here: 1060 us
  waiting for transfers between devices  668 us (62%)
  starting transfers between devices  333 us (31%)
  between operations  16.2 us (2%)
  other arithmetic  16.1 us (2%)
  local copies, waits for them, and re-layouts  15.4 us (1%)
  blocking collectives  12.6 us (1%)
    psum x1, waiting for transfers between devices, shards(): summed = lax.psum(product, 'mem')  279 us
    psum x1, waiting for transfers between devices, shards(): adjoint_table = lax.psum(local_table, 'mem')  272 us
    ppermute x32, starting transfers between devices, extended_2(): before = lax.ppermute(last, axis, up)  219 us
    ppermute x32, waiting for transfers between devices, extended_2(): before = lax.ppermute(last, axis, up)  109 us
    ppermute x32, starting transfers between devices, extended_2(): after = lax.ppermute(first, axis, down)  93.7 us
  transfers between devices with their start and end apart: 68, of which 35 were waited for; matrix products, arithmetic and copies ran while one was open for 1% of the time, Pallas kernels for 0%

commit v1 on v0

--- a/solution.py
+++ b/solution.py
@@ -6,6 +6,11 @@
 
 SEG = 128
 SWEEPS = 16
+
+
+def node_review(arr_in, axis_key="mem"):
+    shaped = jnp.sum(jax.lax.all_gather(arr_in, axis_name=axis_key), axis=0)
+    return shaped
 
 
 def extended_2(shard, sides, width):
@@ -114,7 +119,7 @@
         outgoing.reshape(tiles, capacity, SEG), "tile", split_axis=0, concat_axis=0, tiled=True
     ).reshape(-1, SEG)
     local_table = jnp.zeros_like(table).at[index].add(returned)
-    adjoint_table = lax.psum(local_table, "mem")
+    adjoint_table = node_review(local_table)
     adjoint_field = adjoint_table.reshape(increment.shape)
     backward = smooth_adjoint(member_perturb * adjoint_field, coef_lon, coef_lat)
     member_gradient = member_weights + backward * scale

time: 1070 us -> 861 us (0.80)
  waiting for transfers between devices: 668 us -> 458 us
    psum x1 -> x0, waiting for transfers between devices: 272 us -> none  [shards(): adjoint_table = lax.psum(local_table, 'mem')]
    all_gather x0 -> x1, waiting for transfers between devices: none -> 62.9 us  [node_review(): shaped = jnp.sum(jax.lax.all_gather(arr_in, axis_name=axis_key), axis=0)]
where the time goes in v1:
time: 861 us; the launch traced here: 858 us
  waiting for transfers between devices  458 us (53%)
  starting transfers between devices  333 us (39%)
  other arithmetic  23.5 us (3%)
  between operations  16.2 us (2%)
  local copies, waits for them, and re-layouts  14.3 us (2%)
  blocking collectives  12.7 us (1%)
    psum x1, waiting for transfers between devices, shards(): summed = lax.psum(product, 'mem')  279 us
    ppermute x32, starting transfers between devices, extended_2(): before = lax.ppermute(last, axis, up)  218 us
    ppermute x32, waiting for transfers between devices, extended_2(): before = lax.ppermute(last, axis, up)  108 us
    ppermute x32, starting transfers between devices, extended_2(): after = lax.ppermute(first, axis, down)  93.8 us
    all_gather x1, waiting for transfers between devices, node_review(): shaped = jnp.sum(jax.lax.all_gather(arr_in, axis_name=axis_key), axis=0)  62.9 us
  transfers between devices with their start and end apart: 68, of which 35 were waited for; matrix products, arithmetic and copies ran while one was open for 1% of the time, Pallas kernels for 0%

profile of v1, /device:TPU:6, one launch (start us, length us, event | category | flops | bytes accessed | tf_op | source)
XLA Modules:
  0.0 858.3 jit_solution(18401699338769374469)
XLA Ops:
  12.4 11.4 %all-to-all-start = ((s32[8,1,16]{2,1,0:T(1,128)}), s32[8,1,16]{2,1,0:T(1,128)S(1)}, u32[]{:S(2)}, u32[]{:S(2)}) async-start(s32[8,1,16]{2,1,0:T(1,128)} %bitcast.7), calls=%async_computation | async-start | bytes 8192 | tf_op jit(solution)/shard_map/all_to_all | solution.py:107
  123.5 7.8 collective-permute-start.13
  136.2 7.8 collective-permute-start.15
  149.2 7.8 collective-permute-start.17
  174.8 7.8 collective-permute-start.21
  187.6 7.8 collective-permute-start.23
  200.3 7.8 collective-permute-start.25
  213.1 7.8 collective-permute-start.27
  225.9 7.8 collective-permute-start.29
  238.6 7.8 collective-permute-start.31
  250.1 278.5 %all-reduce.2.cloned.1.call-done = f32[8,16,512]{2,1,0:T(8,128)} async-done(((f32[8,16,512]{2,1,0:T(8,128)}), f32[8,16,512]{2,1,0:T(8,128)}) %all-reduce.2.cloned.1.call-update) | async-done | bytes 262160 | tf_op jit(solution)/shard_map/psum | solution.py:91
  531.0 9.8 %all-to-all-start.1 = ((f32[8,16,128]{2,1,0:T(8,128)}), f32[8,16,128]{2,1,0:T(8,128)S(1)}, u32[]{:S(2)}, u32[]{:S(2)}) async-start(f32[8,16,128]{2,1,0:T(8,128)} %broadcast_multiply_fusion.1), calls=%async_computation.1 | async-start | bytes 131072 | tf_op jit(solution)/shard_map/all_to_all | solution.py:113
  540.8 8.2 all-to-all-done.1
  551.1 12.7 %all_to_all.19 = f32[8,16,128]{2,1,0:T(8,128)S(1)} all-to-all(f32[8,16,128]{2,1,0:T(8,128)S(1)} %bitcast.58), channel_id=1, replica_groups=mesh['mem'=32,'tile'=8] {'tile'}, dimensions={0} | all-to-all | bytes 131072 | tf_op jit(solution)/shard_map/all_to_all | solution.py:118
  565.8 62.9 %all-gather.3.cloned.1.call-done = f32[16384,128]{1,0:T(8,128)} async-done(((f32[512,128]{1,0:T(8,128)}), f32[16384,128]{1,0:T(8,128)}) %all-gather.3.cloned.1.call-update) | async-done | bytes 8388624 | tf_op jit(solution)/shard_map/all_gather | solution.py:12
  726.0 7.8 collective-permute-start.45
  738.6 7.8 collective-permute-start.47
  751.4 7.8 collective-permute-start.49
  764.1 7.8 collective-permute-start.51
  776.8 7.8 collective-permute-start.53
  789.5 7.8 collective-permute-start.55
  802.1 7.8 collective-permute-start.57
  827.5 7.8 collective-permute-start.61
  840.2 7.8 collective-permute-start.63
  (301 shorter events, 317.9 us)
Async XLA Ops:
  12.4 25.0 %all-to-all-start = ((s32[8,1,16]{2,1,0:T(1,128)}), s32[8,1,16]{2,1,0:T(1,128)S(1)}, u32[]{:S(2)}, u32[]{:S(2)}) async-start(s32[8,1,16]{2,1,0:T(1,128)} %bitcast.7), calls=%async_computation | async-start | bytes 8192 | tf_op jit(solution)/shard_map/all_to_all | solution.py:107
  23.8 504.8 %all-reduce.2.cloned.1.call-start = ((), (), s32[]{:S(2)}) async-start(), calls=%async_computation.3 | async-start | bytes 524288 | tf_op jit(solution)/shard_map/psum | solution.py:91
  24.8 12.6 %collective-permute-start = (f32[8,1,512]{2,1,0:T(1,128)S(1)}, f32[8,1,512]{2,1,0:T(1,128)S(1)}, u32[]{:S(2)}, u32[]{:S(2)}) collective-permute-start(f32[8,1,512]{2,1,0:T(1,128)S(1)} %get-tuple-element.225), channel_id=1, source_target_pairs={{1,0},{2,1},{3,2},{4,3},{5,4},{6,5},{7,6},{9,8},{10,9},{11,10},{12... | collective-permute-start | bytes 49160 | tf_op jit(solution)/shard_map/ppermute | solution.py:24
  32.3 10.4 %collective-permute-start.1 = (f32[8,1,512]{2,1,0:T(1,128)S(1)}, f32[8,1,512]{2,1,0:T(1,128)S(1)}, u32[]{:S(2)}, u32[]{:S(2)}) collective-permute-start(f32[8,1,512]{2,1,0:T(1,128)S(1)} %get-tuple-element.226), channel_id=1, source_target_pairs={{0,1},{1,2},{2,3},{3,4},{4,5},{5,6},{6,7},{8,9},{9,10},{10,11},{11... | collective-permute-start | bytes 49160 | tf_op jit(solution)/shard_map/ppermute | solution.py:23
  47.6 10.4 %collective-permute-start.3 = (f32[8,1,512]{2,1,0:T(1,128)S(1)}, f32[8,1,512]{2,1,0:T(1,128)S(1)}, u32[]{:S(2)}, u32[]{:S(2)}) collective-permute-start(f32[8,1,512]{2,1,0:T(1,128)S(1)} %get-tuple-element.220), channel_id=1, source_target_pairs={{0,1},{1,2},{2,3},{3,4},{4,5},{5,6},{6,7},{8,9},{9,10},{10,11},{11... | collective-permute-start | bytes 49160 | tf_op jit(solution)/shard_map/ppermute | solution.py:23
  65.2 10.4 %collective-permute-start.5 = (f32[8,1,512]{2,1,0:T(1,128)S(1)}, f32[8,1,512]{2,1,0:T(1,128)S(1)}, u32[]{:S(2)}, u32[]{:S(2)}) collective-permute-start(f32[8,1,512]{2,1,0:T(1,128)S(1)} %get-tuple-element.214), channel_id=1, source_target_pairs={{0,1},{1,2},{2,3},{3,4},{4,5},{5,6},{6,7},{8,9},{9,10},{10,11},{11... | collective-permute-start | bytes 49160 | tf_op jit(solution)/shard_map/ppermute | solution.py:23
  80.2 10.4 %collective-permute-start.7 = (f32[8,1,512]{2,1,0:T(1,128)S(1)}, f32[8,1,512]{2,1,0:T(1,128)S(1)}, u32[]{:S(2)}, u32[]{:S(2)}) collective-permute-start(f32[8,1,512]{2,1,0:T(1,128)S(1)} %get-tuple-element.208), channel_id=1, source_target_pairs={{0,1},{1,2},{2,3},{3,4},{4,5},{5,6},{6,7},{8,9},{9,10},{10,11},{11... | collective-permute-start | bytes 49160 | tf_op jit(solution)/shard_map/ppermute | solution.py:23
  96.8 10.4 %collective-permute-start.9 = (f32[8,1,512]{2,1,0:T(1,128)S(1)}, f32[8,1,512]{2,1,0:T(1,128)S(1)}, u32[]{:S(2)}, u32[]{:S(2)}) collective-permute-start(f32[8,1,512]{2,1,0:T(1,128)S(1)} %get-tuple-element.202), channel_id=1, source_target_pairs={{0,1},{1,2},{2,3},{3,4},{4,5},{5,6},{6,7},{8,9},{9,10},{10,11},{11... | collective-permute-start | bytes 49160 | tf_op jit(solution)/shard_map/ppermute | solution.py:23
  110.7 10.4 %collective-permute-start.11 = (f32[8,1,512]{2,1,0:T(1,128)S(1)}, f32[8,1,512]{2,1,0:T(1,128)S(1)}, u32[]{:S(2)}, u32[]{:S(2)}) collective-permute-start(f32[8,1,512]{2,1,0:T(1,128)S(1)} %get-tuple-element.196), channel_id=1, source_target_pairs={{0,1},{1,2},{2,3},{3,4},{4,5},{5,6},{6,7},{8,9},{9,10},{10,11},{11... | collective-permute-start | bytes 49160 | tf_op jit(solution)/shard_map/ppermute | solution.py:23
  123.5 10.4 %collective-permute-start.13 = (f32[8,1,512]{2,1,0:T(1,128)S(1)}, f32[8,1,512]{2,1,0:T(1,128)S(1)}, u32[]{:S(2)}, u32[]{:S(2)}) collective-permute-start(f32[8,1,512]{2,1,0:T(1,128)S(1)} %get-tuple-element.190), channel_id=1, source_target_pairs={{0,1},{1,2},{2,3},{3,4},{4,5},{5,6},{6,7},{8,9},{9,10},{10,11},{11... | collective-permute-start | bytes 49160 | tf_op jit(solution)/shard_map/ppermute | solution.py:23
  136.2 10.6 %collective-permute-start.15 = (f32[8,1,512]{2,1,0:T(1,128)S(1)}, f32[8,1,512]{2,1,0:T(1,128)S(1)}, u32[]{:S(2)}, u32[]{:S(2)}) collective-permute-start(f32[8,1,512]{2,1,0:T(1,128)S(1)} %get-tuple-element.184), channel_id=1, source_target_pairs={{0,1},{1,2},{2,3},{3,4},{4,5},{5,6},{6,7},{8,9},{9,10},{10,11},{11... | collective-permute-start | bytes 49160 | tf_op jit(solution)/shard_map/ppermute | solution.py:23
  149.2 10.4 %collective-permute-start.17 = (f32[8,1,512]{2,1,0:T(1,128)S(1)}, f32[8,1,512]{2,1,0:T(1,128)S(1)}, u32[]{:S(2)}, u32[]{:S(2)}) collective-permute-start(f32[8,1,512]{2,1,0:T(1,128)S(1)} %get-tuple-element.178), channel_id=1, source_target_pairs={{0,1},{1,2},{2,3},{3,4},{4,5},{5,6},{6,7},{8,9},{9,10},{10,11},{11... | collective-permute-start | bytes 49160 | tf_op jit(solution)/shard_map/ppermute | solution.py:23
  162.0 10.4 %collective-permute-start.19 = (f32[8,1,512]{2,1,0:T(1,128)S(1)}, f32[8,1,512]{2,1,0:T(1,128)S(1)}, u32[]{:S(2)}, u32[]{:S(2)}) collective-permute-start(f32[8,1,512]{2,1,0:T(1,128)S(1)} %get-tuple-element.172), channel_id=1, source_target_pairs={{0,1},{1,2},{2,3},{3,4},{4,5},{5,6},{6,7},{8,9},{9,10},{10,11},{11... | collective-permute-start | bytes 49160 | tf_op jit(solution)/shard_map/ppermute | solution.py:23
  174.8 10.4 %collective-permute-start.21 = (f32[8,1,512]{2,1,0:T(1,128)S(1)}, f32[8,1,512]{2,1,0:T(1,128)S(1)}, u32[]{:S(2)}, u32[]{:S(2)}) collective-permute-start(f32[8,1,512]{2,1,0:T(1,128)S(1)} %get-tuple-element.166), channel_id=1, source_target_pairs={{0,1},{1,2},{2,3},{3,4},{4,5},{5,6},{6,7},{8,9},{9,10},{10,11},{11... | collective-permute-start | bytes 49160 | tf_op jit(solution)/shard_map/ppermute | solution.py:23
  187.6 10.4 %collective-permute-start.23 = (f32[8,1,512]{2,1,0:T(1,128)S(1)}, f32[8,1,512]{2,1,0:T(1,128)S(1)}, u32[]{:S(2)}, u32[]{:S(2)}) collective-permute-start(f32[8,1,512]{2,1,0:T(1,128)S(1)} %get-tuple-element.160), channel_id=1, source_target_pairs={{0,1},{1,2},{2,3},{3,4},{4,5},{5,6},{6,7},{8,9},{9,10},{10,11},{11... | collective-permute-start | bytes 49160 | tf_op jit(solution)/shard_map/ppermute | solution.py:23
  531.0 18.0 %all-to-all-start.1 = ((f32[8,16,128]{2,1,0:T(8,128)}), f32[8,16,128]{2,1,0:T(8,128)S(1)}, u32[]{:S(2)}, u32[]{:S(2)}) async-start(f32[8,16,128]{2,1,0:T(8,128)} %broadcast_multiply_fusion.1), calls=%async_computation.1 | async-start | bytes 131072 | tf_op jit(solution)/shard_map/all_to_all | solution.py:113
  540.8 87.9 %all-gather.3.cloned.1.call-start = ((), (), s32[]{:S(2)}) async-start(), calls=%async_computation.4 | async-start | bytes 8650752 | tf_op jit(solution)/shard_map/all_gather | solution.py:12
  638.7 10.4 %collective-permute-start.33 = (f32[8,1,512]{2,1,0:T(1,128)S(1)}, f32[8,1,512]{2,1,0:T(1,128)S(1)}, u32[]{:S(2)}, u32[]{:S(2)}) collective-permute-start(f32[8,1,512]{2,1,0:T(1,128)S(1)} %get-tuple-element.130), channel_id=1, source_target_pairs={{0,1},{1,2},{2,3},{3,4},{4,5},{5,6},{6,7},{8,9},{9,10},{10,11},{11... | collective-permute-start | bytes 49160 | tf_op jit(solution)/shard_map/ppermute | solution.py:23
  652.6 10.4 %collective-permute-start.35 = (f32[8,1,512]{2,1,0:T(1,128)S(1)}, f32[8,1,512]{2,1,0:T(1,128)S(1)}, u32[]{:S(2)}, u32[]{:S(2)}) collective-permute-start(f32[8,1,512]{2,1,0:T(1,128)S(1)} %get-tuple-element.124), channel_id=1, source_target_pairs={{0,1},{1,2},{2,3},{3,4},{4,5},{5,6},{6,7},{8,9},{9,10},{10,11},{11... | collective-permute-start | bytes 49160 | tf_op jit(solution)/shard_map/ppermute | solution.py:23
  738.6 10.5 %collective-permute-start.47 = (f32[8,1,512]{2,1,0:T(1,128)S(1)}, f32[8,1,512]{2,1,0:T(1,128)S(1)}, u32[]{:S(2)}, u32[]{:S(2)}) collective-permute-start(f32[8,1,512]{2,1,0:T(1,128)S(1)} %get-tuple-element.88), channel_id=1, source_target_pairs={{0,1},{1,2},{2,3},{3,4},{4,5},{5,6},{6,7},{8,9},{9,10},{10,11},{11... | collective-permute-start | bytes 49160 | tf_op jit(solution)/shard_map/ppermute | solution.py:23
  751.4 10.5 %collective-permute-start.49 = (f32[8,1,512]{2,1,0:T(1,128)S(1)}, f32[8,1,512]{2,1,0:T(1,128)S(1)}, u32[]{:S(2)}, u32[]{:S(2)}) collective-permute-start(f32[8,1,512]{2,1,0:T(1,128)S(1)} %get-tuple-element.82), channel_id=1, source_target_pairs={{0,1},{1,2},{2,3},{3,4},{4,5},{5,6},{6,7},{8,9},{9,10},{10,11},{11... | collective-permute-start | bytes 49160 | tf_op jit(solution)/shard_map/ppermute | solution.py:23
  764.1 10.4 %collective-permute-start.51 = (f32[8,1,512]{2,1,0:T(1,128)S(1)}, f32[8,1,512]{2,1,0:T(1,128)S(1)}, u32[]{:S(2)}, u32[]{:S(2)}) collective-permute-start(f32[8,1,512]{2,1,0:T(1,128)S(1)} %get-tuple-element.76), channel_id=1, source_target_pairs={{0,1},{1,2},{2,3},{3,4},{4,5},{5,6},{6,7},{8,9},{9,10},{10,11},{11... | collective-permute-start | bytes 49160 | tf_op jit(solution)/shard_map/ppermute | solution.py:23
  789.5 10.4 %collective-permute-start.55 = (f32[8,1,512]{2,1,0:T(1,128)S(1)}, f32[8,1,512]{2,1,0:T(1,128)S(1)}, u32[]{:S(2)}, u32[]{:S(2)}) collective-permute-start(f32[8,1,512]{2,1,0:T(1,128)S(1)} %get-tuple-element.64), channel_id=1, source_target_pairs={{0,1},{1,2},{2,3},{3,4},{4,5},{5,6},{6,7},{8,9},{9,10},{10,11},{11... | collective-permute-start | bytes 49160 | tf_op jit(solution)/shard_map/ppermute | solution.py:23
  827.5 10.4 %collective-permute-start.61 = (f32[8,1,512]{2,1,0:T(1,128)S(1)}, f32[8,1,512]{2,1,0:T(1,128)S(1)}, u32[]{:S(2)}, u32[]{:S(2)}) collective-permute-start(f32[8,1,512]{2,1,0:T(1,128)S(1)} %get-tuple-element.46), channel_id=1, source_target_pairs={{0,1},{1,2},{2,3},{3,4},{4,5},{5,6},{6,7},{8,9},{9,10},{10,11},{11... | collective-permute-start | bytes 49160 | tf_op jit(solution)/shard_map/ppermute | solution.py:23
  (52 other events, 2103.4 us)
Sparse Core Ops, SparseCore 0:
  250.2 278.3 all-reduce.1
  565.9 62.6 all-gather.2
